TPU v7x, 128 devices: a whole 4x4x4 slice. The times are simulated.
128 devices in a mesh: ctx: 4 (over z_hi, core), fsdp: 32 (over z_lo, x, y).
Axes of the slice: x: 4, y: 4, z: 4 (z_hi: 2, z_lo: 2; z = z_hi * 2 + z_lo), core: 2. Of those that a mesh axis runs over, the one named last changes fastest.
Arguments:
- query: bfloat16 [2, 8192, 4096], P(None, ('ctx', 'fsdp')), may hold values from -64 to 64
- key: bfloat16 [2, 8192, 2048], P(None, ('ctx', 'fsdp')), may hold values from -32 to 32
- value: bfloat16 [2, 8192, 2048], P(None, ('ctx', 'fsdp')), may hold values from -6 to 6
- grad_out: bfloat16 [2, 8192, 4096], P(None, ('ctx', 'fsdp')), may hold values from -6 to 6
- tile_start: int32 [2, 64], replicated, may hold values from 0 to 63, as said below
Outputs:
- grad_query: bfloat16 [2, 8192, 4096], P(None, ('ctx', 'fsdp'))
- grad_key: bfloat16 [2, 8192, 2048], P(None, ('ctx', 'fsdp'))
- grad_value: bfloat16 [2, 8192, 2048], P(None, ('ctx', 'fsdp'))
Inputs may be any that keep to these rules, and one draw needn't show every extreme that they name: tile_start[b, t] is the first tile of the document holding tile t: it equals t or tile_start[b, t - 1], and tile_start[b, 0] = 0; the last tile of every sequence begins a document; no document begins at a tile whose first token is a nonzero multiple of 2048.
All inputs are finite; a program needn't handle non-finite values.
Results may differ from a plain program's by a relative error of at most 0.012.
Values may be sent and summed in bfloat16 or wider, within the bound.
A program may use at most 64 MiB of HBM per device.

v0:
```python
import functools
import math

import jax
import jax.numpy as jnp
from jax import lax
from jax.experimental import pallas as pl
from jax.experimental.pallas import tpu as pltpu
from jax.sharding import PartitionSpec as P

MESH = pl.DeviceIdType.MESH
F32 = jnp.float32
BF16 = jnp.bfloat16

HEAD = 128
TILE = 128
WINDOW = 1024
SEQS = 2
PEERS = 16
BLOCKS = 8
OWN = 1024
ROWS = OWN // PEERS
TILES = OWN // TILE
SPAN = WINDOW + TILE
EXT = WINDOW + OWN
REACH = WINDOW // TILE + 1
NEG = -1e30

score_scale = 168.0 ** (-0.5)
exp2_scale = score_scale * math.log2(math.e)

NT = (((1,), (1,)), ((), ()))
NN = (((1,), (0,)), ((), ()))

K, V, Q, G = range(4)


def dot(a, b, dims):
    return lax.dot_general(a, b, dims, preferred_element_type=F32)


def rows_of(start, size):
    return pl.ds(pl.multiple_of(start, size), size)


def query_tile(i, s, block, starts, qb, gb, kx, vx, kt, sb, db, pb, tb, dka, dva, dqo):
    here = rows_of(i * TILE, TILE)
    span = pl.ds(pl.multiple_of(i * TILE, TILE), SPAN)
    q = qb[s, here, :]
    g = gb[s, here, :]
    q2 = jnp.concatenate([q[:, :HEAD], q[:, HEAD:]], axis=0)
    g2 = jnp.concatenate([g[:, :HEAD], g[:, HEAD:]], axis=0)
    sb[...] = dot(kx[s, span, :], q2, NT)
    db[...] = dot(vx[s, span, :], g2, NT)
    tile = block * TILES + i
    first = starts[s, tile]
    row = lax.broadcasted_iota(jnp.int32, (TILE, 2 * TILE), 0)
    col = lax.broadcasted_iota(jnp.int32, (TILE, 2 * TILE), 1)
    lower = row <= jnp.where(col < TILE, col, col - TILE)
    sb[:TILE] = jnp.where(lower, NEG, sb[:TILE])
    sb[WINDOW:] = jnp.where(lower, sb[WINDOW:], NEG)
    bias = []
    top = None
    for n in range(REACH):
        part = slice(n * TILE, (n + 1) * TILE)
        bias.append(jnp.where(tile - (REACH - 1) + n >= first, 0.0, NEG).astype(F32))
        high = jnp.max(sb[part].reshape(TILE // 8, 8, 2 * TILE), axis=0) + bias[n]
        top = high if top is None else jnp.maximum(top, high)
    top = jnp.max(top, axis=0, keepdims=True) * exp2_scale
    total = jnp.zeros((8, 2 * TILE), F32)
    delta = jnp.zeros((8, 2 * TILE), F32)
    for n in range(REACH):
        part = slice(n * TILE, (n + 1) * TILE)
        weights = jnp.exp2(sb[part] * exp2_scale - (top - bias[n]))
        total = total + jnp.sum(weights.reshape(TILE // 8, 8, 2 * TILE), axis=0)
        delta = delta + jnp.sum((weights * db[part]).reshape(TILE // 8, 8, 2 * TILE), axis=0)
        sb[part] = weights
    inverse = 1.0 / jnp.sum(total, axis=0, keepdims=True)
    delta = jnp.sum(delta, axis=0, keepdims=True) * inverse
    for n in range(REACH):
        part = slice(n * TILE, (n + 1) * TILE)
        probs = sb[part] * inverse
        pb[part] = probs.astype(BF16)
        tb[part] = (probs * (db[part] - delta)).astype(BF16)
    dva[span, :] += dot(pb[...], g2, NN)
    dka[span, :] += dot(tb[...], q2, NN)
    dq = (dot(kt[:, span], tb[...], NN) * score_scale).T
    dqo[s, here, :HEAD] = dq[:TILE].astype(BF16)
    dqo[s, here, HEAD:] = dq[TILE:].astype(BF16)


def kernel(
    starts, q_ref, k_ref, v_ref, g_ref, dq_ref, dk_ref, dv_ref,
    qb, gb, kx, vx, kt, sb, db, pb, tb, dka, dva, hs, hr, dqo, dko, dvo,
    in_recv, in_send, halo_recv, halo_send, back_recv, back_send, out_recv, out_send,
):
    ctx = lax.axis_index("ctx")
    place = lax.axis_index("fsdp")
    me = lax.rem(place, PEERS)
    half = place // PEERS
    block = ctx * 2 + half
    following = (ctx + half, (1 - half) * PEERS + me)
    previous = (ctx - (1 - half), (1 - half) * PEERS + me)
    has_next = block < BLOCKS - 1
    has_prev = block > 0

    def peer(j):
        x = lax.rem(me // 4 + j // 4, 4)
        y = lax.rem(lax.rem(me, 4) + lax.rem(j, 4), 4)
        return x * 4 + y

    def device(p):
        return (ctx, half * PEERS + p)

    barrier = pltpu.get_barrier_semaphore()

    def greet(j, carry):
        pl.semaphore_signal(barrier, inc=1, device_id=device(peer(j)), device_id_type=MESH)
        return carry

    lax.fori_loop(1, PEERS, greet, 0)

    @pl.when(has_next)
    def _():
        pl.semaphore_signal(barrier, inc=1, device_id=following, device_id_type=MESH)

    @pl.when(has_prev)
    def _():
        pl.semaphore_signal(barrier, inc=1, device_id=previous, device_id_type=MESH)

    more = jnp.where(has_next, 1, 0) + jnp.where(has_prev, 1, 0)
    pl.semaphore_wait(barrier, PEERS - 1 + more)

    incoming = {
        K: (k_ref, lambda s: kx.at[s, pl.ds(WINDOW, OWN), :], HEAD),
        V: (v_ref, lambda s: vx.at[s, pl.ds(WINDOW, OWN), :], HEAD),
        Q: (q_ref, lambda s: qb.at[s], 2 * HEAD),
        G: (g_ref, lambda s: gb.at[s], 2 * HEAD),
    }

    def scatter(s, kind):
        ref, buf, width = incoming[kind]
        landing = buf(s).at[rows_of(me * ROWS, ROWS), :]

        def columns(p):
            return ref.at[s, :, rows_of(p * width, width)]

        pltpu.make_async_copy(columns(me), landing, in_recv.at[s, kind]).start()

        def send(j, carry):
            p = peer(j)
            pltpu.make_async_remote_copy(
                columns(p), landing, in_send.at[s, kind], in_recv.at[s, kind],
                device_id=device(p), device_id_type=MESH,
            ).start()
            return carry

        lax.fori_loop(1, PEERS, send, 0)

    for s, kind in ((0, K), (0, V), (1, K), (1, V), (0, Q), (0, G), (1, Q), (1, G)):
        scatter(s, kind)

    @pl.when(jnp.logical_not(has_prev))
    def _():
        kx[:, :WINDOW, :] = jnp.zeros((SEQS, WINDOW, HEAD), BF16)
        vx[:, :WINDOW, :] = jnp.zeros((SEQS, WINDOW, HEAD), BF16)

    @pl.when(jnp.logical_not(has_next))
    def _():
        hr[...] = jnp.zeros_like(hr)

    def arrived(ref, sem):
        pltpu.make_async_copy(ref, ref, sem).wait()

    def forward(s):
        for kind, buf in ((K, kx), (V, vx)):
            own = buf.at[s, pl.ds(WINDOW, OWN), :]
            arrived(own, in_recv.at[s, kind])

            @pl.when(has_next)
            def _():
                pltpu.make_async_remote_copy(
                    own, buf.at[s, pl.ds(0, WINDOW), :], halo_send.at[s, kind], halo_recv.at[s, kind],
                    device_id=following, device_id_type=MESH,
                ).start()

    def compute(s):
        arrived(qb.at[s], in_recv.at[s, Q])
        arrived(gb.at[s], in_recv.at[s, G])
        dka[...] = jnp.zeros_like(dka)
        dva[...] = jnp.zeros_like(dva)

        @pl.when(has_prev)
        def _():
            for kind, buf in ((K, kx), (V, vx)):
                arrived(buf.at[s, pl.ds(0, WINDOW), :], halo_recv.at[s, kind])

        def turn(t, carry):
            part = rows_of(t * TILE, TILE)
            kt[:, part] = kx[s, part, :].T
            return carry

        lax.fori_loop(0, EXT // TILE, turn, 0)

        def step(i, carry):
            query_tile(i, s, block, starts, qb, gb, kx, vx, kt, sb, db, pb, tb, dka, dva, dqo)
            part = rows_of(i * TILE, TILE)
            hs[s, 0, part, :] = (dka[part, :] * score_scale).astype(BF16)
            hs[s, 1, part, :] = dva[part, :].astype(BF16)

            @pl.when(has_prev)
            def _():
                for n in range(2):
                    pltpu.make_async_remote_copy(
                        hs.at[s, n, part, :], hr.at[s, n, part, :], back_send.at[s, n], back_recv.at[s, n],
                        device_id=previous, device_id_type=MESH,
                    ).start()

            return carry

        lax.fori_loop(0, TILES, step, 0)

    def outgoing(s, kind, buf, ref, width):
        columns = ref.at[s, :, rows_of(me * width, width)]
        pltpu.make_async_copy(buf.at[s, rows_of(me * ROWS, ROWS), :], columns, out_recv.at[s, kind]).start()

        def send(j, carry):
            p = peer(j)
            pltpu.make_async_remote_copy(
                buf.at[s, rows_of(p * ROWS, ROWS), :], columns, out_send.at[s, kind], out_recv.at[s, kind],
                device_id=device(p), device_id_type=MESH,
            ).start()
            return carry

        lax.fori_loop(1, PEERS, send, 0)

    forward(0)
    forward(1)
    for s in range(SEQS):
        compute(s)
        outgoing(s, 0, dqo, dq_ref, 2 * HEAD)

        @pl.when(has_next)
        def _():
            for n in range(2):
                arrived(hr.at[s, n], back_recv.at[s, n])

        dko[s] = (dka[WINDOW:, :] * score_scale + hr[s, 0].astype(F32)).astype(BF16)
        dvo[s] = (dva[WINDOW:, :] + hr[s, 1].astype(F32)).astype(BF16)
        outgoing(s, 1, dko, dk_ref, HEAD)
        outgoing(s, 2, dvo, dv_ref, HEAD)

    others = OWN - ROWS
    for s in range(SEQS):
        for kind, ref in ((0, dq_ref), (1, dk_ref), (2, dv_ref)):
            arrived(ref.at[s], out_recv.at[s, kind])
        for kind, buf in ((0, dqo), (1, dko), (2, dvo)):
            arrived(buf.at[s, pl.ds(0, others), :], out_send.at[s, kind])
        for kind, (_, buf, _) in incoming.items():
            arrived(buf(s).at[pl.ds(0, others), :], in_send.at[s, kind])

        @pl.when(has_next)
        def _():
            for kind, buf in ((K, kx), (V, vx)):
                arrived(buf.at[s, pl.ds(0, WINDOW), :], halo_send.at[s, kind])

        @pl.when(has_prev)
        def _():
            for n in range(2):
                arrived(hs.at[s, n], back_send.at[s, n])


def body(query, key, value, grad_out, tile_start):
    dma = pltpu.SemaphoreType.DMA
    hbm = pl.BlockSpec(memory_space=pl.ANY)
    return pl.pallas_call(
        kernel,
        out_shape=(
            jax.ShapeDtypeStruct(query.shape, BF16),
            jax.ShapeDtypeStruct(key.shape, BF16),
            jax.ShapeDtypeStruct(value.shape, BF16),
        ),
        in_specs=[pl.BlockSpec(memory_space=pltpu.SMEM)] + [hbm] * 4,
        out_specs=[hbm] * 3,
        scratch_shapes=[
            pltpu.VMEM((SEQS, OWN, 2 * HEAD), BF16),
            pltpu.VMEM((SEQS, OWN, 2 * HEAD), BF16),
            pltpu.VMEM((SEQS, EXT, HEAD), BF16),
            pltpu.VMEM((SEQS, EXT, HEAD), BF16),
            pltpu.VMEM((HEAD, EXT), BF16),
            pltpu.VMEM((SPAN, 2 * TILE), F32),
            pltpu.VMEM((SPAN, 2 * TILE), F32),
            pltpu.VMEM((SPAN, 2 * TILE), BF16),
            pltpu.VMEM((SPAN, 2 * TILE), BF16),
            pltpu.VMEM((EXT, HEAD), F32),
            pltpu.VMEM((EXT, HEAD), F32),
            pltpu.VMEM((SEQS, 2, WINDOW, HEAD), BF16),
            pltpu.VMEM((SEQS, 2, WINDOW, HEAD), BF16),
            pltpu.VMEM((SEQS, OWN, 2 * HEAD), BF16),
            pltpu.VMEM((SEQS, OWN, HEAD), BF16),
            pltpu.VMEM((SEQS, OWN, HEAD), BF16),
            dma((SEQS, 4)), dma((SEQS, 4)),
            dma((SEQS, 2)), dma((SEQS, 2)),
            dma((SEQS, 2)), dma((SEQS, 2)),
            dma((SEQS, 3)), dma((SEQS, 3)),
        ],
        compiler_params=pltpu.CompilerParams(
            collective_id=0, has_side_effects=True, vmem_limit_bytes=48 * 2**20
        ),
        name="attention_grads",
    )(tile_start, query, key, value, grad_out)


def solution(mesh):
    spread = P(None, ("ctx", "fsdp"), None)
    return jax.shard_map(
        body, mesh=mesh, in_specs=(spread,) * 4 + (P(),), out_specs=(spread,) * 3, check_vma=False
    )
```

profile of v0, /device:TPU:0, one launch (start us, length us, event | category | flops | bytes accessed | tf_op | source)
XLA Modules:
  0.0 86.4 jit_solution(16358844500056823985)
XLA Ops:
  0.6 0.0 copy-start
  0.6 1.2 %copy-done = bf16[2,64,4096]{2,1,0:T(8,128)(2,1)S(1)} copy-done((bf16[2,64,4096]{2,1,0:T(8,128)(2,1)S(1)}, bf16[2,64,4096]{2,1,0:T(8,128)(2,1)}, u32[]{:S(2)}) %copy-start) | copy-done | bytes 1048600
  1.9 0.0 copy-start.1
  1.9 1.2 %copy-done.1 = bf16[2,64,4096]{2,1,0:T(8,128)(2,1)S(1)} copy-done((bf16[2,64,4096]{2,1,0:T(8,128)(2,1)S(1)}, bf16[2,64,4096]{2,1,0:T(8,128)(2,1)}, u32[]{:S(2)}) %copy-start.1) | copy-done | bytes 1048600
  3.1 0.0 copy-start.2
  3.1 1.0 %copy-done.2 = bf16[2,64,2048]{2,1,0:T(8,128)(2,1)S(1)} copy-done((bf16[2,64,2048]{2,1,0:T(8,128)(2,1)S(1)}, bf16[2,64,2048]{2,1,0:T(8,128)(2,1)}, u32[]{:S(2)}) %copy-start.2) | copy-done | bytes 524312
  4.1 0.0 copy-start.3
  4.1 1.0 %copy-done.3 = bf16[2,64,2048]{2,1,0:T(8,128)(2,1)S(1)} copy-done((bf16[2,64,2048]{2,1,0:T(8,128)(2,1)S(1)}, bf16[2,64,2048]{2,1,0:T(8,128)(2,1)}, u32[]{:S(2)}) %copy-start.3) | copy-done | bytes 524312
  5.2 0.0 copy-start.4
  5.2 0.7 copy-done.4
  5.8 78.0 %attention_grads.1 = (bf16[2,64,4096]{2,1,0:T(8,128)(2,1)S(1)}, bf16[2,64,2048]{2,1,0:T(8,128)(2,1)S(1)}, bf16[2,64,2048]{2,1,0:T(8,128)(2,1)S(1)}) custom-call(s32[2,64]{1,0:T(2,128)S(1)} %copy-done.4, bf16[2,64,4096]{2,1,0:T(8,128)(2,1)S(1)} %copy-done, bf16[2,64,2048]{2,1,0:T(8,128)(2,1)S(1)} %copy-done.2, bf16[2,64,2048]{2,1,0:T(8,128)(2,1)S(1)} %copy-done.3, ...), custom_call_target="tpu_custom_call" | custom-call | tf_op jit(solution)/shard_map/attention_grads/pallas_call | solution.py:276
  83.8 1.0 %copy.11 = bf16[2,64,4096]{2,1,0:T(8,128)(2,1)} copy(bf16[2,64,4096]{2,1,0:T(8,128)(2,1)S(1)} %get-tuple-element.6) | data formatting | bytes 2097152
  84.8 0.8 copy.12
  85.6 0.8 copy.13
Async XLA Ops:
  0.6 1.2 %copy-start = (bf16[2,64,4096]{2,1,0:T(8,128)(2,1)S(1)}, bf16[2,64,4096]{2,1,0:T(8,128)(2,1)}, u32[]{:S(2)}) copy-start(bf16[2,64,4096]{2,1,0:T(8,128)(2,1)} %q_ref.1) | copy-start | bytes 3145732
  1.9 1.2 %copy-start.1 = (bf16[2,64,4096]{2,1,0:T(8,128)(2,1)S(1)}, bf16[2,64,4096]{2,1,0:T(8,128)(2,1)}, u32[]{:S(2)}) copy-start(bf16[2,64,4096]{2,1,0:T(8,128)(2,1)} %g_ref.1) | copy-start | bytes 3145732
  3.1 1.0 %copy-start.2 = (bf16[2,64,2048]{2,1,0:T(8,128)(2,1)S(1)}, bf16[2,64,2048]{2,1,0:T(8,128)(2,1)}, u32[]{:S(2)}) copy-start(bf16[2,64,2048]{2,1,0:T(8,128)(2,1)} %k_ref.1) | copy-start | bytes 1572868
  4.1 1.0 %copy-start.3 = (bf16[2,64,2048]{2,1,0:T(8,128)(2,1)S(1)}, bf16[2,64,2048]{2,1,0:T(8,128)(2,1)}, u32[]{:S(2)}) copy-start(bf16[2,64,2048]{2,1,0:T(8,128)(2,1)} %v_ref.1) | copy-start | bytes 1572868
  5.2 0.7 copy-start.4
where the time goes:
time: 87.5 us; the launch traced here: 86.4 us
  Pallas kernels  78 us (89%)
  local copies, waits for them, and re-layouts  7.76 us (9%)
    pallas_call x1, Pallas kernels, body(): pl.pallas_call(kernel, out_shape=(jax.ShapeDtypeStruct(query.shape, BF16)...  78 us
    unnamed x13, local copies, waits for them, and re-layouts  7.76 us

commit v1 on v0

v1 whole, which is shorter than its diff:
```python
import functools
import math

import jax
import jax.numpy as jnp
from jax import lax
from jax.experimental import pallas as pl
from jax.experimental.pallas import tpu as pltpu
from jax.sharding import PartitionSpec as P

MESH = pl.DeviceIdType.MESH
F32 = jnp.float32
BF16 = jnp.bfloat16

HEAD = 128
TILE = 128
WINDOW = 1024
SEQS = 2
PEERS = 16
BLOCKS = 8
OWN = 1024
ROWS = OWN // PEERS
TILES = OWN // TILE
QUERIES = 256
STEPS = OWN // QUERIES
LATE = 1
EDGE = QUERIES // TILE
SPAN = WINDOW + QUERIES
EXT = WINDOW + OWN
NEG = -1e30

score_scale = 168.0 ** (-0.5)
exp2_scale = score_scale * math.log2(math.e)

NT = (((1,), (1,)), ((), ()))
NN = (((1,), (0,)), ((), ()))

K, V, Q, G = range(4)
ARRIVALS = (
    [(s, kind) for s in range(SEQS) for kind in (K, V)]
    + [(s, kind + 2 * h) for s in range(SEQS) for h in range(2) for kind in (Q, G)]
)


def dot(a, b, dims):
    return lax.dot_general(a, b, dims, preferred_element_type=F32)


def rows_of(start, size):
    return pl.ds(pl.multiple_of(start, size), size)


def fold(x):
    return x.reshape(x.shape[0] // 8, 8, QUERIES)


def lower_of(n):
    row = lax.broadcasted_iota(jnp.int32, (TILE, QUERIES), 0) + n * TILE
    return row <= lax.broadcasted_iota(jnp.int32, (TILE, QUERIES), 1)


def query_step(i, s, h, block, starts, qb, gb, kx, vx, kt, sb, db, pb, tb, dka, dva, dqo):
    here = rows_of(i * QUERIES, QUERIES)
    span = pl.ds(pl.multiple_of(i * QUERIES, QUERIES), SPAN)
    q = qb[s, h, here, :]
    g = gb[s, h, here, :]
    sb[...] = dot(kx[s, span, :], q, NT)
    db[...] = dot(vx[s, span, :], g, NT)
    lane = lax.broadcasted_iota(jnp.int32, (1, QUERIES), 1)
    tile = block * TILES + 2 * i
    first = [starts[s, tile], starts[s, tile + 1]]
    bias = []
    for n in range(SPAN // TILE):
        key_tile = tile - WINDOW // TILE + n
        seen = [jnp.where(key_tile >= f, 0.0, NEG).astype(F32) for f in first]
        bias.append(jnp.where(lane < TILE, seen[0], seen[1]))
    top = None
    for n in range(WINDOW // TILE):
        part = slice(n * TILE, (n + 1) * TILE)
        if n < EDGE:
            lower = lower_of(n)
            near = slice(WINDOW + n * TILE, WINDOW + (n + 1) * TILE)
            merged = jnp.where(lower, sb[near] + bias[WINDOW // TILE + n], sb[part] + bias[n])
            sb[part] = merged
            db[part] = jnp.where(lower, db[near], db[part])
            high = jnp.max(fold(merged), axis=0)
        else:
            high = jnp.max(fold(sb[part]), axis=0) + bias[n]
        top = high if top is None else jnp.maximum(top, high)
    top = jnp.max(top, axis=0, keepdims=True) * exp2_scale
    total = jnp.zeros((8, QUERIES), F32)
    delta = jnp.zeros((8, QUERIES), F32)
    for n in range(WINDOW // TILE):
        part = slice(n * TILE, (n + 1) * TILE)
        weights = jnp.exp2(sb[part] * exp2_scale - (top if n < EDGE else top - bias[n]))
        total = total + jnp.sum(fold(weights), axis=0)
        delta = delta + jnp.sum(fold(weights * db[part]), axis=0)
        sb[part] = weights
    inverse = 1.0 / jnp.sum(total, axis=0, keepdims=True)
    delta = jnp.sum(delta, axis=0, keepdims=True) * inverse
    for n in range(WINDOW // TILE):
        part = slice(n * TILE, (n + 1) * TILE)
        probs = sb[part] * inverse
        grads = probs * (db[part] - delta)
        if n < EDGE:
            lower = lower_of(n)
            near = slice(WINDOW + n * TILE, WINDOW + (n + 1) * TILE)
            pb[near] = jnp.where(lower, probs, 0.0).astype(BF16)
            tb[near] = jnp.where(lower, grads, 0.0).astype(BF16)
            pb[part] = jnp.where(lower, 0.0, probs).astype(BF16)
            tb[part] = jnp.where(lower, 0.0, grads).astype(BF16)
        else:
            pb[part] = probs.astype(BF16)
            tb[part] = grads.astype(BF16)
    dva[s, span, :] += dot(pb[...], g, NN)
    dka[s, span, :] += dot(tb[...], q, NN)
    dqo[s, h, here, :] = (dot(kt[:, span], tb[...], NN) * score_scale).T.astype(BF16)


def kernel(
    starts, q_ref, k_ref, v_ref, g_ref, dq_ref, dk_ref, dv_ref,
    qb, gb, kx, vx, kt, sb, db, pb, tb, dka, dva, hs, hr, dqo, dko, dvo,
    in_recv, in_send, halo_recv, halo_send, back_recv, back_send, out_recv, out_send,
):
    ctx = lax.axis_index("ctx")
    place = lax.axis_index("fsdp")
    me = lax.rem(place, PEERS)
    half = place // PEERS
    block = ctx * 2 + half
    following = (ctx + half, (1 - half) * PEERS + me)
    previous = (ctx - (1 - half), (1 - half) * PEERS + me)
    has_next = block < BLOCKS - 1
    has_prev = block > 0

    def peer(j):
        x = lax.rem(me // 4 + j // 4, 4)
        y = lax.rem(lax.rem(me, 4) + lax.rem(j, 4), 4)
        return x * 4 + y

    def device(p):
        return (ctx, half * PEERS + p)

    barrier = pltpu.get_barrier_semaphore()

    def greet(j, carry):
        pl.semaphore_signal(barrier, inc=1, device_id=device(peer(j)), device_id_type=MESH)
        return carry

    lax.fori_loop(1, PEERS, greet, 0)

    @pl.when(has_next)
    def _():
        pl.semaphore_signal(barrier, inc=1, device_id=following, device_id_type=MESH)

    @pl.when(has_prev)
    def _():
        pl.semaphore_signal(barrier, inc=1, device_id=previous, device_id_type=MESH)

    more = jnp.where(has_next, 1, 0) + jnp.where(has_prev, 1, 0)
    pl.semaphore_wait(barrier, PEERS - 1 + more)

    def keys_of(ref, buf):
        def source(s, p):
            return ref.at[s, :, rows_of(p * HEAD, HEAD)]

        return source, lambda s: buf.at[s, pl.ds(WINDOW, OWN), :]

    def heads_of(ref, buf, h):
        def source(s, p):
            return ref.at[s, :, rows_of((2 * p + h) * HEAD, HEAD)]

        return source, lambda s: buf.at[s, h]

    incoming = {
        K: keys_of(k_ref, kx),
        V: keys_of(v_ref, vx),
        Q: heads_of(q_ref, qb, 0),
        G: heads_of(g_ref, gb, 0),
        Q + 2: heads_of(q_ref, qb, 1),
        G + 2: heads_of(g_ref, gb, 1),
    }

    def scatter(s, kind):
        source, buf = incoming[kind]
        landing = buf(s).at[rows_of(me * ROWS, ROWS), :]
        pltpu.make_async_copy(source(s, me), landing, in_recv.at[s, kind]).start()

        def send(j, carry):
            p = peer(j)
            pltpu.make_async_remote_copy(
                source(s, p), landing, in_send.at[s, kind], in_recv.at[s, kind],
                device_id=device(p), device_id_type=MESH,
            ).start()
            return carry

        lax.fori_loop(1, PEERS, send, 0)

    for s, kind in ARRIVALS:
        scatter(s, kind)

    @pl.when(jnp.logical_not(has_prev))
    def _():
        kx[:, :WINDOW, :] = jnp.zeros((SEQS, WINDOW, HEAD), BF16)
        vx[:, :WINDOW, :] = jnp.zeros((SEQS, WINDOW, HEAD), BF16)

    @pl.when(jnp.logical_not(has_next))
    def _():
        hr[...] = jnp.zeros_like(hr)

    def arrived(ref, sem):
        pltpu.make_async_copy(ref, ref, sem).wait()

    def forward(s):
        for kind, buf in ((K, kx), (V, vx)):
            own = buf.at[s, pl.ds(WINDOW, OWN), :]
            arrived(own, in_recv.at[s, kind])

            @pl.when(has_next)
            def _():
                pltpu.make_async_remote_copy(
                    own, buf.at[s, pl.ds(0, WINDOW), :], halo_send.at[s, kind], halo_recv.at[s, kind],
                    device_id=following, device_id_type=MESH,
                ).start()

    def outgoing(s, kind, buf, columns):
        pltpu.make_async_copy(buf.at[rows_of(me * ROWS, ROWS), :], columns, out_recv.at[s, kind]).start()

        def send(j, carry):
            p = peer(j)
            pltpu.make_async_remote_copy(
                buf.at[rows_of(p * ROWS, ROWS), :], columns, out_send.at[s, kind], out_recv.at[s, kind],
                device_id=device(p), device_id_type=MESH,
            ).start()
            return carry

        lax.fori_loop(1, PEERS, send, 0)

    mine = rows_of(me * HEAD, HEAD)

    def finish(s):
        @pl.when(has_next)
        def _():
            for n in range(2):
                arrived(hr.at[s, n], back_recv.at[s, n])

        dko[s] = (dka[s, WINDOW:, :] * score_scale + hr[s, 0].astype(F32)).astype(BF16)
        outgoing(s, 2, dko.at[s], dk_ref.at[s, :, mine])
        dvo[s] = (dva[s, WINDOW:, :] + hr[s, 1].astype(F32)).astype(BF16)
        outgoing(s, 3, dvo.at[s], dv_ref.at[s, :, mine])

    def compute(s):
        dka[s] = jnp.zeros((EXT, HEAD), F32)
        dva[s] = jnp.zeros((EXT, HEAD), F32)

        @pl.when(has_prev)
        def _():
            for kind, buf in ((K, kx), (V, vx)):
                arrived(buf.at[s, pl.ds(0, WINDOW), :], halo_recv.at[s, kind])

        def turn(t, carry):
            part = rows_of(t * TILE, TILE)
            kt[:, part] = kx[s, part, :].T
            return carry

        lax.fori_loop(0, EXT // TILE, turn, 0)

        def head(h, carry):
            arrived(qb.at[s, h], in_recv.at[s, Q + 2 * h])
            arrived(gb.at[s, h], in_recv.at[s, G + 2 * h])

            def step(i, inner):
                query_step(i, s, h, block, starts, qb, gb, kx, vx, kt, sb, db, pb, tb, dka, dva, dqo)

                @pl.when(h == 1)
                def _():
                    part = rows_of(i * QUERIES, QUERIES)
                    hs[s, 0, part, :] = (dka[s, part, :] * score_scale).astype(BF16)
                    hs[s, 1, part, :] = dva[s, part, :].astype(BF16)

                    @pl.when(has_prev)
                    def _():
                        for n in range(2):
                            pltpu.make_async_remote_copy(
                                hs.at[s, n, part, :], hr.at[s, n, part, :], back_send.at[s, n], back_recv.at[s, n],
                                device_id=previous, device_id_type=MESH,
                            ).start()

                if s > 0:
                    @pl.when(jnp.logical_and(h == 1, i == LATE))
                    def _():
                        finish(s - 1)

                return inner

            lax.fori_loop(0, STEPS, step, 0)
            outgoing(s, h, dqo.at[s, h], dq_ref.at[s, :, rows_of((2 * me + h) * HEAD, HEAD)])
            return carry

        lax.fori_loop(0, 2, head, 0)

    forward(0)
    forward(1)
    compute(0)
    compute(1)
    finish(1)

    others = pl.ds(0, OWN - ROWS)
    for s in range(SEQS):
        for h in range(2):
            arrived(dq_ref.at[s, :, pl.ds(0, PEERS * HEAD)], out_recv.at[s, h])
        arrived(dk_ref.at[s], out_recv.at[s, 2])
        arrived(dv_ref.at[s], out_recv.at[s, 3])
        for kind, buf in enumerate((dqo.at[s, 0], dqo.at[s, 1], dko.at[s], dvo.at[s])):
            arrived(buf.at[others, :], out_send.at[s, kind])
        for kind, (_, buf) in incoming.items():
            arrived(buf(s).at[others, :], in_send.at[s, kind])

        @pl.when(has_next)
        def _():
            for kind, buf in ((K, kx), (V, vx)):
                arrived(buf.at[s, pl.ds(0, WINDOW), :], halo_send.at[s, kind])

        @pl.when(has_prev)
        def _():
            for n in range(2):
                arrived(hs.at[s, n], back_send.at[s, n])


def body(query, key, value, grad_out, tile_start):
    dma = pltpu.SemaphoreType.DMA
    hbm = pl.BlockSpec(memory_space=pl.ANY)
    return pl.pallas_call(
        kernel,
        out_shape=(
            jax.ShapeDtypeStruct(query.shape, BF16),
            jax.ShapeDtypeStruct(key.shape, BF16),
            jax.ShapeDtypeStruct(value.shape, BF16),
        ),
        in_specs=[pl.BlockSpec(memory_space=pltpu.SMEM)] + [hbm] * 4,
        out_specs=[hbm] * 3,
        scratch_shapes=[
            pltpu.VMEM((SEQS, 2, OWN, HEAD), BF16),
            pltpu.VMEM((SEQS, 2, OWN, HEAD), BF16),
            pltpu.VMEM((SEQS, EXT, HEAD), BF16),
            pltpu.VMEM((SEQS, EXT, HEAD), BF16),
            pltpu.VMEM((HEAD, EXT), BF16),
            pltpu.VMEM((SPAN, QUERIES), F32),
            pltpu.VMEM((SPAN, QUERIES), F32),
            pltpu.VMEM((SPAN, QUERIES), BF16),
            pltpu.VMEM((SPAN, QUERIES), BF16),
            pltpu.VMEM((SEQS, EXT, HEAD), F32),
            pltpu.VMEM((SEQS, EXT, HEAD), F32),
            pltpu.VMEM((SEQS, 2, WINDOW, HEAD), BF16),
            pltpu.VMEM((SEQS, 2, WINDOW, HEAD), BF16),
            pltpu.VMEM((SEQS, 2, OWN, HEAD), BF16),
            pltpu.VMEM((SEQS, OWN, HEAD), BF16),
            pltpu.VMEM((SEQS, OWN, HEAD), BF16),
            dma((SEQS, 6)), dma((SEQS, 6)),
            dma((SEQS, 2)), dma((SEQS, 2)),
            dma((SEQS, 2)), dma((SEQS, 2)),
            dma((SEQS, 4)), dma((SEQS, 4)),
        ],
        compiler_params=pltpu.CompilerParams(
            collective_id=0, has_side_effects=True, vmem_limit_bytes=67043328
        ),
        name="attention_grads",
    )(tile_start, query, key, value, grad_out)


def solution(mesh):
    spread = P(None, ("ctx", "fsdp"), None)
    return jax.shard_map(
        body, mesh=mesh, in_specs=(spread,) * 4 + (P(),), out_specs=(spread,) * 3, check_vma=False
    )
```

time: 87.5 us -> 75.3 us (0.86); the launches traced: 86.4 us -> 75.1 us
  Pallas kernels: 78 us -> 70 us
  local copies, waits for them, and re-layouts: 7.76 us -> 4.37 us
    pallas_call x1, Pallas kernels: 78 us -> 70 us  [body(): pl.pallas_call(kernel, out_shape=(jax.ShapeDtypeStruct(query.shape, BF16)...]
    unnamed x13 -> x7, local copies, waits for them, and re-layouts: 7.76 us -> 4.37 us
where the time goes in v1:
time: 75.3 us; the launch traced here: 75.1 us
  Pallas kernels  70 us (93%)
  local copies, waits for them, and re-layouts  4.37 us (6%)
    pallas_call x1, Pallas kernels, body(): pl.pallas_call(kernel, out_shape=(jax.ShapeDtypeStruct(query.shape, BF16)...  70 us
    unnamed x7, local copies, waits for them, and re-layouts  4.37 us

profile of v1, /device:TPU:0, one launch (start us, length us, event | category | flops | bytes accessed | tf_op | source)
XLA Modules:
  0.0 75.1 jit_solution(10288905134314919812)
XLA Ops:
  0.6 70.0 %attention_grads.1 = (bf16[2,64,4096]{2,1,0:T(8,128)(2,1)}, bf16[2,64,2048]{2,1,0:T(8,128)(2,1)}, bf16[2,64,2048]{2,1,0:T(8,128)(2,1)}) custom-call(s32[2,64]{1,0:T(2,128)} %starts.1, bf16[2,64,4096]{2,1,0:T(8,128)(2,1)} %q_ref.1, bf16[2,64,2048]{2,1,0:T(8,128)(2,1)} %k_ref.1, bf16[2,64,2048]{2,1,0:T(8,128)(2,1)} %v_ref.1, bf16[2,64,4096]{2,1,0:T(8,128)(2,1)} %g_ref.1), custom_call_target="tpu_custom_call" | custom-call | tf_op jit(solution)/shard_map/attention_grads/pallas_call | solution.py:332
  70.7 0.0 copy-start.1
  70.7 2.3 %copy.11 = bf16[2,64,4096]{2,1,0:T(8,128)(2,1)} copy(bf16[2,64,4096]{2,1,0:T(8,128)(2,1)} %get-tuple-element.6) | data formatting | bytes 2097152
  73.0 0.0 copy-done.1
  73.0 0.0 copy-start
  73.0 0.8 %copy.12 = bf16[2,64,2048]{2,1,0:T(8,128)(2,1)} copy(bf16[2,64,2048]{2,1,0:T(8,128)(2,1)S(1)} %copy-done.1) | data formatting | bytes 1048576
  73.8 0.4 copy-done
  74.3 0.8 %copy.13 = bf16[2,64,2048]{2,1,0:T(8,128)(2,1)} copy(bf16[2,64,2048]{2,1,0:T(8,128)(2,1)S(1)} %copy-done) | data formatting | bytes 1048576
Async XLA Ops:
  70.7 2.4 %copy-start.1 = (bf16[2,64,2048]{2,1,0:T(8,128)(2,1)S(1)}, bf16[2,64,2048]{2,1,0:T(8,128)(2,1)}, u32[]{:S(2)}) copy-start(bf16[2,64,2048]{2,1,0:T(8,128)(2,1)} %get-tuple-element.7) | copy-start | bytes 1572868
  73.0 1.2 %copy-start = (bf16[2,64,2048]{2,1,0:T(8,128)(2,1)S(1)}, bf16[2,64,2048]{2,1,0:T(8,128)(2,1)}, u32[]{:S(2)}) copy-start(bf16[2,64,2048]{2,1,0:T(8,128)(2,1)} %get-tuple-element.8) | copy-start | bytes 1572868

commit v2 on v1

--- a/solution.py
+++ b/solution.py
@@ -329,12 +329,12 @@
 def body(query, key, value, grad_out, tile_start):
     dma = pltpu.SemaphoreType.DMA
     hbm = pl.BlockSpec(memory_space=pl.ANY)
-    return pl.pallas_call(
+    grads = pl.pallas_call(
         kernel,
         out_shape=(
-            jax.ShapeDtypeStruct(query.shape, BF16),
-            jax.ShapeDtypeStruct(key.shape, BF16),
-            jax.ShapeDtypeStruct(value.shape, BF16),
+            pltpu.VMEM(query.shape, BF16),
+            pltpu.VMEM(key.shape, BF16),
+            pltpu.VMEM(value.shape, BF16),
         ),
         in_specs=[pl.BlockSpec(memory_space=pltpu.SMEM)] + [hbm] * 4,
         out_specs=[hbm] * 3,
@@ -361,10 +361,36 @@
             dma((SEQS, 4)), dma((SEQS, 4)),
         ],
         compiler_params=pltpu.CompilerParams(
-            collective_id=0, has_side_effects=True, vmem_limit_bytes=67043328
+            collective_id=0, has_side_effects=True, vmem_limit_bytes=64400000
         ),
         name="attention_grads",
     )(tile_start, query, key, value, grad_out)
+    return placed(grads)
+
+
+def place(dq_in, dk_in, dv_in, dq_out, dk_out, dv_out, left):
+    copies = [
+        pltpu.make_async_copy(ref, out, left.at[n])
+        for n, (ref, out) in enumerate(((dq_in, dq_out), (dk_in, dk_out), (dv_in, dv_out)))
+    ]
+    for copy in copies:
+        copy.start()
+    for copy in copies:
+        copy.wait()
+
+
+def placed(grads):
+    dma = pltpu.SemaphoreType.DMA
+    hbm = pl.BlockSpec(memory_space=pl.ANY)
+    return pl.pallas_call(
+        place,
+        out_shape=tuple(jax.ShapeDtypeStruct(g.shape, g.dtype) for g in grads),
+        in_specs=[hbm] * 3,
+        out_specs=[hbm] * 3,
+        scratch_shapes=[dma((3,))],
+        compiler_params=pltpu.CompilerParams(vmem_limit_bytes=2**20),
+        name="place_grads",
+    )(*grads)
 
 
 def solution(mesh):

time: 75.3 us -> 72.1 us (0.958)
  local copies, waits for them, and re-layouts: 4.37 us -> 0 us
  Pallas kernels: 70 us -> 71.3 us
    unnamed x7 -> x0, local copies, waits for them, and re-layouts: 4.37 us -> none
    pallas_call x1 -> x2, Pallas kernels: 70 us -> 71.3 us  [the longest x1 70 us: body(): pl.pallas_call(kernel, out_shape=(pltpu.VMEM(query.shape, BF16), pltpu.VM...]
where the time goes in v2:
time: 72.1 us; the launch traced here: 72 us
  Pallas kernels  71.3 us (99%)
    pallas_call x1, Pallas kernels, body(): pl.pallas_call(kernel, out_shape=(pltpu.VMEM(query.shape, BF16), pltpu.VM...  70 us

profile of v2, /device:TPU:0, one launch (start us, length us, event | category | flops | bytes accessed | tf_op | source)
XLA Modules:
  0.0 72.0 jit_solution(11299103097905059070)
XLA Ops:
  0.6 70.0 %attention_grads.1 = (bf16[2,64,4096]{2,1,0:T(8,128)(2,1)S(1)}, bf16[2,64,2048]{2,1,0:T(8,128)(2,1)S(1)}, bf16[2,64,2048]{2,1,0:T(8,128)(2,1)S(1)}) custom-call(s32[2,64]{1,0:T(2,128)} %starts.1, bf16[2,64,4096]{2,1,0:T(8,128)(2,1)} %q_ref.1, bf16[2,64,2048]{2,1,0:T(8,128)(2,1)} %k_ref.1, bf16[2,64,2048]{2,1,0:T(8,128)(2,1)} %v_ref.1, bf16[2,64,4096]{2,1,0:T(8,128)(2,1)} %g_ref.1), custom_call_target="tpu_custom_call" | custom-call | tf_op jit(solution)/shard_map/attention_grads/pallas_call | solution.py:332
  70.6 1.3 %place_grads.1 = (bf16[2,64,4096]{2,1,0:T(8,128)(2,1)}, bf16[2,64,2048]{2,1,0:T(8,128)(2,1)}, bf16[2,64,2048]{2,1,0:T(8,128)(2,1)}) custom-call(bf16[2,64,4096]{2,1,0:T(8,128)(2,1)S(1)} %get-tuple-element.6.dq_in, bf16[2,64,2048]{2,1,0:T(8,128)(2,1)S(1)} %get-tuple-element.7.dk_in, bf16[2,64,2048]{2,1,0:T(8,128)(2,1)S(1)} %get-tuple-element.8.dv_in), custom_call_target="tpu_custom_call" | custom-call | tf_op jit(solution)/shard_map/place_grads/pallas_call | solution.py:385

commit v3 on v2

--- a/solution.py
+++ b/solution.py
@@ -59,16 +59,20 @@
     return row <= lax.broadcasted_iota(jnp.int32, (TILE, QUERIES), 1)
 
 
-def query_step(i, s, h, block, starts, qb, gb, kx, vx, kt, sb, db, pb, tb, dka, dva, dqo):
-    here = rows_of(i * QUERIES, QUERIES)
-    span = pl.ds(pl.multiple_of(i * QUERIES, QUERIES), SPAN)
-    q = qb[s, h, here, :]
-    g = gb[s, h, here, :]
-    sb[...] = dot(kx[s, span, :], q, NT)
-    db[...] = dot(vx[s, span, :], g, NT)
+def spans(i):
+    return pl.ds(i * QUERIES, QUERIES), pl.ds(i * QUERIES, SPAN)
+
+
+def scores(i, q, g, keys, values, sb, db):
+    here, span = spans(i)
+    sb[...] = dot(keys[span, :], q[here, :], NT)
+    db[...] = dot(values[span, :], g[here, :], NT)
+
+
+def score_grads(i, starts, block, sb, db, pb, tb):
     lane = lax.broadcasted_iota(jnp.int32, (1, QUERIES), 1)
-    tile = block * TILES + 2 * i
-    first = [starts[s, tile], starts[s, tile + 1]]
+    tile = block * TILES + EDGE * i
+    first = [starts[tile], starts[tile + 1]]
     bias = []
     for n in range(SPAN // TILE):
         key_tile = tile - WINDOW // TILE + n
@@ -112,14 +116,11 @@
         else:
             pb[part] = probs.astype(BF16)
             tb[part] = grads.astype(BF16)
-    dva[s, span, :] += dot(pb[...], g, NN)
-    dka[s, span, :] += dot(tb[...], q, NN)
-    dqo[s, h, here, :] = (dot(kt[:, span], tb[...], NN) * score_scale).T.astype(BF16)
 
 
 def kernel(
     starts, q_ref, k_ref, v_ref, g_ref, dq_ref, dk_ref, dv_ref,
-    qb, gb, kx, vx, kt, sb, db, pb, tb, dka, dva, hs, hr, dqo, dko, dvo,
+    qb, gb, kx, vx, kt, sb, db, sb2, db2, pb, tb, dka, dva, hs, hr, dqo, dko, dvo,
     in_recv, in_send, halo_recv, halo_send, back_recv, back_send, out_recv, out_send,
 ):
     ctx = lax.axis_index("ctx")
@@ -127,10 +128,8 @@
     me = lax.rem(place, PEERS)
     half = place // PEERS
     block = ctx * 2 + half
-    following = (ctx + half, (1 - half) * PEERS + me)
-    previous = (ctx - (1 - half), (1 - half) * PEERS + me)
-    has_next = block < BLOCKS - 1
-    has_prev = block > 0
+    following = (lax.rem(ctx + half, BLOCKS // 2), (1 - half) * PEERS + me)
+    previous = (lax.rem(ctx + half + BLOCKS // 2 - 1, BLOCKS // 2), (1 - half) * PEERS + me)
 
     def peer(j):
         x = lax.rem(me // 4 + j // 4, 4)
@@ -148,16 +147,9 @@
 
     lax.fori_loop(1, PEERS, greet, 0)
 
-    @pl.when(has_next)
-    def _():
-        pl.semaphore_signal(barrier, inc=1, device_id=following, device_id_type=MESH)
-
-    @pl.when(has_prev)
-    def _():
-        pl.semaphore_signal(barrier, inc=1, device_id=previous, device_id_type=MESH)
-
-    more = jnp.where(has_next, 1, 0) + jnp.where(has_prev, 1, 0)
-    pl.semaphore_wait(barrier, PEERS - 1 + more)
+    for neighbour in (following, previous):
+        pl.semaphore_signal(barrier, inc=1, device_id=neighbour, device_id_type=MESH)
+    pl.semaphore_wait(barrier, PEERS + 1)
 
     def keys_of(ref, buf):
         def source(s, p):
@@ -198,29 +190,28 @@
     for s, kind in ARRIVALS:
         scatter(s, kind)
 
-    @pl.when(jnp.logical_not(has_prev))
-    def _():
-        kx[:, :WINDOW, :] = jnp.zeros((SEQS, WINDOW, HEAD), BF16)
-        vx[:, :WINDOW, :] = jnp.zeros((SEQS, WINDOW, HEAD), BF16)
-
-    @pl.when(jnp.logical_not(has_next))
-    def _():
-        hr[...] = jnp.zeros_like(hr)
+    dka[...] = jnp.zeros_like(dka)
+    dva[...] = jnp.zeros_like(dva)
 
     def arrived(ref, sem):
         pltpu.make_async_copy(ref, ref, sem).wait()
+
+    def turn(s, start):
+        def one(t, carry):
+            part = rows_of(start + t * TILE, TILE)
+            kt[s, :, part] = kx[s, part, :].T
+            return carry
+
+        lax.fori_loop(0, OWN // TILE, one, 0)
 
     def forward(s):
         for kind, buf in ((K, kx), (V, vx)):
             own = buf.at[s, pl.ds(WINDOW, OWN), :]
             arrived(own, in_recv.at[s, kind])
-
-            @pl.when(has_next)
-            def _():
-                pltpu.make_async_remote_copy(
-                    own, buf.at[s, pl.ds(0, WINDOW), :], halo_send.at[s, kind], halo_recv.at[s, kind],
-                    device_id=following, device_id_type=MESH,
-                ).start()
+            pltpu.make_async_remote_copy(
+                own, buf.at[s, pl.ds(0, WINDOW), :], halo_send.at[s, kind], halo_recv.at[s, kind],
+                device_id=following, device_id_type=MESH,
+            ).start()
 
     def outgoing(s, kind, buf, columns):
         pltpu.make_async_copy(buf.at[rows_of(me * ROWS, ROWS), :], columns, out_recv.at[s, kind]).start()
@@ -238,71 +229,51 @@
     mine = rows_of(me * HEAD, HEAD)
 
     def finish(s):
-        @pl.when(has_next)
-        def _():
-            for n in range(2):
-                arrived(hr.at[s, n], back_recv.at[s, n])
-
+        arrived(hr.at[s, 0], back_recv.at[s, 0])
         dko[s] = (dka[s, WINDOW:, :] * score_scale + hr[s, 0].astype(F32)).astype(BF16)
         outgoing(s, 2, dko.at[s], dk_ref.at[s, :, mine])
+        arrived(hr.at[s, 1], back_recv.at[s, 1])
         dvo[s] = (dva[s, WINDOW:, :] + hr[s, 1].astype(F32)).astype(BF16)
         outgoing(s, 3, dvo.at[s], dv_ref.at[s, :, mine])
 
-    def compute(s):
-        dka[s] = jnp.zeros((EXT, HEAD), F32)
-        dva[s] = jnp.zeros((EXT, HEAD), F32)
-
-        @pl.when(has_prev)
-        def _():
-            for kind, buf in ((K, kx), (V, vx)):
-                arrived(buf.at[s, pl.ds(0, WINDOW), :], halo_recv.at[s, kind])
-
-        def turn(t, carry):
-            part = rows_of(t * TILE, TILE)
-            kt[:, part] = kx[s, part, :].T
-            return carry
-
-        lax.fori_loop(0, EXT // TILE, turn, 0)
-
-        def head(h, carry):
-            arrived(qb.at[s, h], in_recv.at[s, Q + 2 * h])
-            arrived(gb.at[s, h], in_recv.at[s, G + 2 * h])
-
-            def step(i, inner):
-                query_step(i, s, h, block, starts, qb, gb, kx, vx, kt, sb, db, pb, tb, dka, dva, dqo)
-
-                @pl.when(h == 1)
-                def _():
-                    part = rows_of(i * QUERIES, QUERIES)
-                    hs[s, 0, part, :] = (dka[s, part, :] * score_scale).astype(BF16)
-                    hs[s, 1, part, :] = dva[s, part, :].astype(BF16)
-
-                    @pl.when(has_prev)
-                    def _():
-                        for n in range(2):
-                            pltpu.make_async_remote_copy(
-                                hs.at[s, n, part, :], hr.at[s, n, part, :], back_send.at[s, n], back_recv.at[s, n],
-                                device_id=previous, device_id_type=MESH,
-                            ).start()
-
-                if s > 0:
-                    @pl.when(jnp.logical_and(h == 1, i == LATE))
-                    def _():
-                        finish(s - 1)
-
-                return inner
-
-            lax.fori_loop(0, STEPS, step, 0)
-            outgoing(s, h, dqo.at[s, h], dq_ref.at[s, :, rows_of((2 * me + h) * HEAD, HEAD)])
-            return carry
-
-        lax.fori_loop(0, 2, head, 0)
-
-    forward(0)
-    forward(1)
-    compute(0)
-    compute(1)
-    finish(1)
+    scratch = ((sb, db), (sb2, db2))
+
+    def unit(s, h):
+        arrived(qb.at[s, h], in_recv.at[s, Q + 2 * h])
+        arrived(gb.at[s, h], in_recv.at[s, G + 2 * h])
+        q, g = qb.at[s, h], gb.at[s, h]
+        scores(0, q, g, kx.at[s], vx.at[s], *scratch[0])
+        for i in range(STEPS):
+            here, span = spans(i)
+            if i + 1 < STEPS:
+                scores(i + 1, q, g, kx.at[s], vx.at[s], *scratch[(i + 1) % 2])
+            score_grads(i, starts.at[s], block, *scratch[i % 2], pb, tb)
+            dva[s, span, :] += dot(pb[...], g[here, :], NN)
+            dka[s, span, :] += dot(tb[...], q[here, :], NN)
+            if h == 1:
+                hs[s, 0, here, :] = (dka[s, here, :] * score_scale).astype(BF16)
+                hs[s, 1, here, :] = dva[s, here, :].astype(BF16)
+            dqo[s, h, here, :] = (dot(kt[s, :, span], tb[...], NN) * score_scale).T.astype(BF16)
+            if h == 1:
+                for n in range(2):
+                    pltpu.make_async_remote_copy(
+                        hs.at[s, n, here, :], hr.at[s, n, here, :], back_send.at[s, n], back_recv.at[s, n],
+                        device_id=previous, device_id_type=MESH,
+                    ).start()
+            if s > 0 and h == 1 and i == LATE:
+                finish(s - 1)
+        outgoing(s, h, dqo.at[s, h], dq_ref.at[s, :, rows_of((2 * me + h) * HEAD, HEAD)])
+
+    for s in range(SEQS):
+        forward(s)
+        turn(s, WINDOW)
+    for s in range(SEQS):
+        for kind, buf in ((K, kx), (V, vx)):
+            arrived(buf.at[s, pl.ds(0, WINDOW), :], halo_recv.at[s, kind])
+        turn(s, 0)
+        for h in range(2):
+            unit(s, h)
+    finish(SEQS - 1)
 
     others = pl.ds(0, OWN - ROWS)
     for s in range(SEQS):
@@ -315,15 +286,10 @@
         for kind, (_, buf) in incoming.items():
             arrived(buf(s).at[others, :], in_send.at[s, kind])
 
-        @pl.when(has_next)
-        def _():
-            for kind, buf in ((K, kx), (V, vx)):
-                arrived(buf.at[s, pl.ds(0, WINDOW), :], halo_send.at[s, kind])
-
-        @pl.when(has_prev)
-        def _():
-            for n in range(2):
-                arrived(hs.at[s, n], back_send.at[s, n])
+        for kind, buf in ((K, kx), (V, vx)):
+            arrived(buf.at[s, pl.ds(0, WINDOW), :], halo_send.at[s, kind])
+        for n in range(2):
+            arrived(hs.at[s, n], back_send.at[s, n])
 
 
 def body(query, key, value, grad_out, tile_start):
@@ -343,7 +309,9 @@
             pltpu.VMEM((SEQS, 2, OWN, HEAD), BF16),
             pltpu.VMEM((SEQS, EXT, HEAD), BF16),
             pltpu.VMEM((SEQS, EXT, HEAD), BF16),
-            pltpu.VMEM((HEAD, EXT), BF16),
+            pltpu.VMEM((SEQS, HEAD, EXT), BF16),
+            pltpu.VMEM((SPAN, QUERIES), F32),
+            pltpu.VMEM((SPAN, QUERIES), F32),
             pltpu.VMEM((SPAN, QUERIES), F32),
             pltpu.VMEM((SPAN, QUERIES), F32),
             pltpu.VMEM((SPAN, QUERIES), BF16),

time: 72.1 us -> 69.2 us (0.960)
  Pallas kernels: 71.3 us -> 68.3 us
    pallas_call x1, Pallas kernels: 70 us -> 66.9 us  [body(): pl.pallas_call(kernel, out_shape=(pltpu.VMEM(query.shape, BF16), pltpu.VM...]
where the time goes in v3:
time: 69.2 us; the launch traced here: 69.1 us
  Pallas kernels  68.3 us (99%)
  between operations  0.8 us (1%)
    pallas_call x1, Pallas kernels, body(): pl.pallas_call(kernel, out_shape=(pltpu.VMEM(query.shape, BF16), pltpu.VM...  66.9 us

profile of v3, /device:TPU:0, one launch (start us, length us, event | category | flops | bytes accessed | tf_op | source)
XLA Modules:
  0.0 69.1 jit_solution(2317180033567426206)
XLA Ops:
  0.6 66.9 %attention_grads.1 = (bf16[2,64,4096]{2,1,0:T(8,128)(2,1)S(1)}, bf16[2,64,2048]{2,1,0:T(8,128)(2,1)S(1)}, bf16[2,64,2048]{2,1,0:T(8,128)(2,1)S(1)}) custom-call(s32[2,64]{1,0:T(2,128)} %starts.1, bf16[2,64,4096]{2,1,0:T(8,128)(2,1)} %q_ref.1, bf16[2,64,2048]{2,1,0:T(8,128)(2,1)} %k_ref.1, bf16[2,64,2048]{2,1,0:T(8,128)(2,1)} %v_ref.1, bf16[2,64,4096]{2,1,0:T(8,128)(2,1)} %g_ref.1), custom_call_target="tpu_custom_call" | custom-call | tf_op jit(solution)/shard_map/attention_grads/pallas_call | solution.py:298
  67.6 1.3 %place_grads.1 = (bf16[2,64,4096]{2,1,0:T(8,128)(2,1)}, bf16[2,64,2048]{2,1,0:T(8,128)(2,1)}, bf16[2,64,2048]{2,1,0:T(8,128)(2,1)}) custom-call(bf16[2,64,4096]{2,1,0:T(8,128)(2,1)S(1)} %get-tuple-element.6.dq_in, bf16[2,64,2048]{2,1,0:T(8,128)(2,1)S(1)} %get-tuple-element.7.dk_in, bf16[2,64,2048]{2,1,0:T(8,128)(2,1)S(1)} %get-tuple-element.8.dv_in), custom_call_target="tpu_custom_call" | custom-call | tf_op jit(solution)/shard_map/place_grads/pallas_call | solution.py:353

commit v4 on v3

--- a/solution.py
+++ b/solution.py
@@ -17,6 +17,7 @@
 WINDOW = 1024
 SEQS = 2
 PEERS = 16
+OTHERS = (10, 9, 11, 6, 14, 8, 2, 5, 7, 13, 15, 1, 3, 4, 12)
 BLOCKS = 8
 OWN = 1024
 ROWS = OWN // PEERS
@@ -133,8 +134,12 @@
 
     def peer(j):
         x = lax.rem(me // 4 + j // 4, 4)
-        y = lax.rem(lax.rem(me, 4) + lax.rem(j, 4), 4)
+        y = lax.rem(lax.rem(me, 4) + j % 4, 4)
         return x * 4 + y
+
+    def for_others(action):
+        for j in OTHERS:
+            action(j, 0)
 
     def device(p):
         return (ctx, half * PEERS + p)
@@ -145,7 +150,7 @@
         pl.semaphore_signal(barrier, inc=1, device_id=device(peer(j)), device_id_type=MESH)
         return carry
 
-    lax.fori_loop(1, PEERS, greet, 0)
+    for_others(greet)
 
     for neighbour in (following, previous):
         pl.semaphore_signal(barrier, inc=1, device_id=neighbour, device_id_type=MESH)
@@ -185,7 +190,7 @@
             ).start()
             return carry
 
-        lax.fori_loop(1, PEERS, send, 0)
+        for_others(send)
 
     for s, kind in ARRIVALS:
         scatter(s, kind)
@@ -224,7 +229,7 @@
             ).start()
             return carry
 
-        lax.fori_loop(1, PEERS, send, 0)
+        for_others(send)
 
     mine = rows_of(me * HEAD, HEAD)
 

time: 69.2 us -> 67.9 us (0.981)
  Pallas kernels: 68.3 us -> 66.9 us
    pallas_call x1, Pallas kernels: 66.9 us -> 65.5 us  [body(): pl.pallas_call(kernel, out_shape=(pltpu.VMEM(query.shape, BF16), pltpu.VM...]
where the time goes in v4:
time: 67.9 us; the launch traced here: 67.7 us
  Pallas kernels  66.9 us (99%)
  between operations  0.8 us (1%)
    pallas_call x1, Pallas kernels, body(): pl.pallas_call(kernel, out_shape=(pltpu.VMEM(query.shape, BF16), pltpu.VM...  65.5 us

profile of v4, /device:TPU:0, one launch (start us, length us, event | category | flops | bytes accessed | tf_op | source)
XLA Modules:
  0.0 67.7 jit_solution(10974050043996536289)
XLA Ops:
  0.6 65.5 %attention_grads.1 = (bf16[2,64,4096]{2,1,0:T(8,128)(2,1)S(1)}, bf16[2,64,2048]{2,1,0:T(8,128)(2,1)S(1)}, bf16[2,64,2048]{2,1,0:T(8,128)(2,1)S(1)}) custom-call(s32[2,64]{1,0:T(2,128)} %starts.1, bf16[2,64,4096]{2,1,0:T(8,128)(2,1)} %q_ref.1, bf16[2,64,2048]{2,1,0:T(8,128)(2,1)} %k_ref.1, bf16[2,64,2048]{2,1,0:T(8,128)(2,1)} %v_ref.1, bf16[2,64,4096]{2,1,0:T(8,128)(2,1)} %g_ref.1), custom_call_target="tpu_custom_call" | custom-call | tf_op jit(solution)/shard_map/attention_grads/pallas_call | solution.py:303
  66.2 1.3 %place_grads.1 = (bf16[2,64,4096]{2,1,0:T(8,128)(2,1)}, bf16[2,64,2048]{2,1,0:T(8,128)(2,1)}, bf16[2,64,2048]{2,1,0:T(8,128)(2,1)}) custom-call(bf16[2,64,4096]{2,1,0:T(8,128)(2,1)S(1)} %get-tuple-element.6.dq_in, bf16[2,64,2048]{2,1,0:T(8,128)(2,1)S(1)} %get-tuple-element.7.dk_in, bf16[2,64,2048]{2,1,0:T(8,128)(2,1)S(1)} %get-tuple-element.8.dv_in), custom_call_target="tpu_custom_call" | custom-call | tf_op jit(solution)/shard_map/place_grads/pallas_call | solution.py:358

commit v5 on v4

--- a/solution.py
+++ b/solution.py
@@ -236,9 +236,9 @@
     def finish(s):
         arrived(hr.at[s, 0], back_recv.at[s, 0])
         dko[s] = (dka[s, WINDOW:, :] * score_scale + hr[s, 0].astype(F32)).astype(BF16)
-        outgoing(s, 2, dko.at[s], dk_ref.at[s, :, mine])
         arrived(hr.at[s, 1], back_recv.at[s, 1])
         dvo[s] = (dva[s, WINDOW:, :] + hr[s, 1].astype(F32)).astype(BF16)
+        outgoing(s, 2, dko.at[s], dk_ref.at[s, :, mine])
         outgoing(s, 3, dvo.at[s], dv_ref.at[s, :, mine])
 
     scratch = ((sb, db), (sb2, db2))

time: 67.9 us -> 67.9 us (level)
  no operation moved by 1% of the time
where the time goes in v5:
time: 67.9 us; the launch traced here: 67.7 us
  Pallas kernels  66.9 us (99%)
  between operations  0.8 us (1%)
    pallas_call x1, Pallas kernels, body(): pl.pallas_call(kernel, out_shape=(pltpu.VMEM(query.shape, BF16), pltpu.VM...  65.5 us

profile of v5, /device:TPU:0, one launch (start us, length us, event | category | flops | bytes accessed | tf_op | source)
XLA Modules:
  0.0 67.7 jit_solution(2650803016817091875)
XLA Ops:
  0.6 65.5 %attention_grads.1 = (bf16[2,64,4096]{2,1,0:T(8,128)(2,1)S(1)}, bf16[2,64,2048]{2,1,0:T(8,128)(2,1)S(1)}, bf16[2,64,2048]{2,1,0:T(8,128)(2,1)S(1)}) custom-call(s32[2,64]{1,0:T(2,128)} %starts.1, bf16[2,64,4096]{2,1,0:T(8,128)(2,1)} %q_ref.1, bf16[2,64,2048]{2,1,0:T(8,128)(2,1)} %k_ref.1, bf16[2,64,2048]{2,1,0:T(8,128)(2,1)} %v_ref.1, bf16[2,64,4096]{2,1,0:T(8,128)(2,1)} %g_ref.1), custom_call_target="tpu_custom_call" | custom-call | tf_op jit(solution)/shard_map/attention_grads/pallas_call | solution.py:303
  66.2 1.3 %place_grads.1 = (bf16[2,64,4096]{2,1,0:T(8,128)(2,1)}, bf16[2,64,2048]{2,1,0:T(8,128)(2,1)}, bf16[2,64,2048]{2,1,0:T(8,128)(2,1)}) custom-call(bf16[2,64,4096]{2,1,0:T(8,128)(2,1)S(1)} %get-tuple-element.6.dq_in, bf16[2,64,2048]{2,1,0:T(8,128)(2,1)S(1)} %get-tuple-element.7.dk_in, bf16[2,64,2048]{2,1,0:T(8,128)(2,1)S(1)} %get-tuple-element.8.dv_in), custom_call_target="tpu_custom_call" | custom-call | tf_op jit(solution)/shard_map/place_grads/pallas_call | solution.py:358
